TPU v7x, 512 devices: a whole 4x8x8 slice. The times are simulated.
512 devices in a mesh: row: 8 (over z), col: 16 (over y, core), vox: 4 (over x).
Axes of the slice: x: 4, y: 8, z: 8, core: 2. Of those that a mesh axis runs over, the one named last changes fastest.
Arguments:
- panel_top: bfloat16 [1024, 1024], P('row', ('col', 'vox')), may hold values from -0.059814453 to 0.059814453
- panel_low: bfloat16 [8192, 1024], P('row', ('col', 'vox')), may hold values from -1.1953125 to 1.1953125
- panel_next: bfloat16 [8192, 1024], P('row', ('col', 'vox')), may hold values from -1.1953125 to 1.1953125
- gram_rest: bfloat16 [8192, 8192], P('row', ('col', 'vox')), may hold values from -18 to 18
- inverses: bfloat16 [2, 1024, 1024], P(None, 'row'), as said below
- right_top: bfloat16 [2, 1024, 8192], P(None, None, ('col', 'vox')), may hold values from -1.796875 to 1.796875
- right_low: bfloat16 [8192, 8192], P('row', ('col', 'vox')), may hold values from -24 to 24
Outputs:
- factor: bfloat16 [2, 8192, 1024], P(None, 'row', ('col', 'vox'))
- solved: bfloat16 [2, 1024, 8192], P(None, None, ('col', 'vox'))
- trailing: float32 [8192, 8192], P('row', ('col', 'vox'))
- residual: float32 [8192, 8192], P('row', ('col', 'vox'))
Inputs may be any that keep to these rules, and one draw needn't show every extreme that they name: Each inverses[k] is lower triangular with diagonal entries from 1 to 2.
All inputs are finite; a program needn't handle non-finite values.
Results may differ from a plain program's by a relative error of at most 0.0057.
Values may be sent and summed in bfloat16 or wider, within the bound.
No kernel may reach another device: no remote copies, remote signals or barrier semaphores. Data moves between devices by JAX's collectives and lax.ppermute only.
A program may use at most 64 MiB of HBM per device.

v0:
```python
import jax
import jax.numpy as jnp
import numpy as np
from jax import lax
from jax.sharding import Mesh
from jax.sharding import PartitionSpec as P


def contract(left, right, dims):
    return lax.dot_general(left, right, (dims, ((), ())), preferred_element_type=jnp.float32)


def gather_small(block, axis, size):
    out = lax.all_to_all(jnp.tile(block, (size, 1)), axis, 0, 0, tiled=True)
    return out.reshape((size,) + block.shape)


def per_device(sizes, panel_top, panel_low, panel_next, gram_rest, inverses, right_top, right_low):
    rows, ys, cores, voxes = sizes
    axes = ("row", "y", "core", "vox")
    order = np.arange(rows * ys * cores * voxes).reshape(sizes)
    swap = list(zip(order.ravel().tolist(), order.transpose(1, 0, 2, 3).ravel().tolist()))
    y = lax.axis_index("y")
    core = lax.axis_index("core")
    vox = lax.axis_index("vox")
    width = panel_low.shape[1]
    rest_cols = gram_rest.shape[1]
    bf16 = jnp.bfloat16
    whole = lax.all_gather(inverses, "row", axis=1, tiled=True)
    top = gather_small(panel_top.T, "row", rows).transpose(1, 0, 2).reshape(width, -1)
    panels = jnp.stack([top, panel_low.T, panel_next.T])
    panels = lax.all_gather(panels, ("y", "core", "vox"), axis=1, tiled=True)
    low = panels[0:2].transpose(1, 0, 2).reshape(panels.shape[1], -1)
    first = contract(whole[0], low, ((1,), (0,))).astype(bf16)
    first_top, first_low = (first[:, : panels.shape[2]], first[:, panels.shape[2] :])
    updated = (panels[2].astype(jnp.float32) - contract(first_top, first_low, ((0,), (0,)))).astype(
        bf16
    )
    second_low = contract(whole[1], updated, ((1,), (0,))).astype(bf16)
    start = (core * voxes + vox) * rest_cols
    first_rows = lax.ppermute(lax.dynamic_slice_in_dim(first_low, start, rest_cols, 1), axes, swap)
    second_rows = lax.ppermute(
        lax.dynamic_slice_in_dim(second_low, start, rest_cols, 1), axes, swap
    )
    first_solve = contract(whole[0], right_top[0], ((1,), (0,))).astype(bf16)
    top_new = (
        right_top[1].astype(jnp.float32) - contract(first_top, first_solve, ((0,), (0,)))
    ).astype(bf16)
    second_solve = contract(whole[1], top_new, ((1,), (0,))).astype(bf16)
    residual = (
        right_low.astype(jnp.float32)
        - contract(first_low, first_solve, ((0,), (0,)))
        - contract(second_low, second_solve, ((0,), (0,)))
    )
    trailing = (
        gram_rest.astype(jnp.float32)
        - contract(first_low, first_rows, ((0,), (0,)))
        - contract(second_low, second_rows, ((0,), (0,)))
    )
    own = ((y * cores + core) * voxes + vox) * width
    factor = jnp.stack(
        [
            lax.dynamic_slice_in_dim(first_low, own, width, 0).T,
            lax.dynamic_slice_in_dim(second_low, own, width, 0).T,
        ]
    )
    solved = jnp.stack([first_solve, second_solve])
    return (factor, solved, trailing, residual)


def solution(mesh):
    cores = 2
    sizes = (mesh.shape["row"], mesh.shape["col"] // cores, cores, mesh.shape["vox"])
    split = Mesh(mesh.devices.reshape(sizes), ("row", "y", "core", "vox"))
    cols = ("y", "core", "vox")
    in_specs = (
        P("row", cols),
        P("row", cols),
        P("row", cols),
        P("row", cols),
        P(None, "row", None),
        P(None, None, cols),
        P("row", cols),
    )
    out_specs = (P(None, "row", cols), P(None, None, cols), P("row", cols), P("row", cols))

    def body(*args):
        return per_device(sizes, *args)

    return jax.shard_map(body, mesh=split, in_specs=in_specs, out_specs=out_specs, check_vma=False)
```

profile of v0, /device:TPU:16, one launch (start us, length us, event | category | flops | bytes accessed | tf_op | source)
XLA Modules:
  0.0 259.9 jit_solution(18153763955404550325)
XLA Ops:
  8.6 18.1 %all_to_all.6 = bf16[8,16,128]{2,1,0:T(8,128)(2,1)S(1)} all-to-all(bf16[8,16,128]{2,1,0:T(8,128)(2,1)S(1)} %tile.2), channel_id=1, replica_groups=mesh['row'=8,'y'=8,'core'=2,'vox'=4] {'row'}, dimensions={0} | all-to-all | bytes 65536 | tf_op jit(solution)/shard_map/all_to_all | solution.py:14
  26.8 1.4 pad_maximum_fusion.1
  28.3 44.6 %all-gather.5.cloned.1.call-done = bf16[2,1024,1024]{2,1,0:T(8,128)(2,1)} async-done(((bf16[2,128,1024]{2,1,0:T(8,128)(2,1)}), bf16[2,1024,1024]{2,1,0:T(8,128)(2,1)}) %all-gather.5.cloned.1.call-update) | async-done | bytes 4194320 | tf_op jit(solution)/shard_map/all_gather | solution.py:29
  72.9 2.3 fusion.17
  75.2 85.2 %all-gather.3.cloned.1.call-done = bf16[3,1024,1024]{2,1,0:T(8,128)(2,1)} async-done(((bf16[3,16,1024]{2,1,0:T(8,128)(2,1)}), bf16[3,1024,1024]{2,1,0:T(8,128)(2,1)}) %all-gather.3.cloned.1.call-update) | async-done | bytes 6291472 | tf_op jit(solution)/shard_map/all_gather | solution.py:32
  160.4 4.7 %slice.34 = bf16[2,1024,1024]{2,1,0:T(8,128)(2,1)} slice(bf16[3,1024,1024]{2,1,0:T(8,128)(2,1)} %all-gather.3.cloned.1.call-done), slice={[0:2], [0:1024], [0:1024]} | slice | bytes 8388608 | tf_op jit(solution)/shard_map/slice | solution.py:33
  165.1 6.2 %copy.22 = bf16[2,1024,1024]{1,2,0:T(8,128)(2,1)} copy(bf16[2,1024,1024]{2,1,0:T(8,128)(2,1)} %slice.34) | data formatting | bytes 8388608
  171.3 7.4 %convert_bitcast_fusion = bf16[1024,2048]{1,0:T(8,128)(2,1)S(1)} fusion(bf16[1024,2048]{0,1:T(8,128)(2,1)} %bitcast.62, bf16[2,1024,1024]{2,1,0:T(8,128)(2,1)} %all-gather.5.cloned.1.call-done), kind=kOutput, calls=%fused_computation.2 | convolution fusion | flops 4297064448 | bytes 10485760 | tf_op jit(solution)/shard_map/dot_general | solution.py:10
  178.7 2.0 copy-done
  180.7 1.5 slice.36
  182.2 8.0 %fusion.3 = bf16[1024,1024]{0,1:T(8,128)(2,1)S(1)} fusion(bf16[3,1024,1024]{2,1,0:T(8,128)(2,1)} %all-gather.3.cloned.1.call-done, bf16[2,1024,1024]{2,1,0:T(8,128)(2,1)} %all-gather.5.cloned.1.call-done, bf16[1024,2048]{1,0:T(8,128)(2,1)} %copy-done), kind=kOutput, calls=%fused_computation.7 | convolution fusion | flops 4299161600 | bytes 10485760 | tf_op jit(solution)/shard_map/dot_general | solution.py:10
  190.2 0.8 dynamic-slice_bitcast_fusion.2
  191.0 0.8 dynamic-slice_bitcast_fusion
  191.8 1.0 constant_dynamic-slice_fusion
  192.8 5.5 %collective-permute-start.1 = (bf16[1024,128]{1,0:T(8,128)(2,1)}, bf16[1024,128]{1,0:T(8,128)(2,1)S(1)}, u32[]{:S(2)}, u32[]{:S(2)}) collective-permute-start(bf16[1024,128]{1,0:T(8,128)(2,1)} %dynamic-slice_bitcast_fusion), channel_id=1, source_target_pairs={{0,0},{1,1},{2,2},{3,3},{4,4},{5,5},{6,6},{7,7},{8,64},{9,65},{10,... | collective-permute-start | bytes 786440 | tf_op jit(solution)/shard_map/ppermute | solution.py:42
  198.2 3.2 %collective-permute-start = (bf16[1024,128]{1,0:T(8,128)(2,1)S(1)}, bf16[1024,128]{1,0:T(8,128)(2,1)}, u32[]{:S(2)}, u32[]{:S(2)}) collective-permute-start(bf16[1024,128]{1,0:T(8,128)(2,1)S(1)} %constant_dynamic-slice_fusion), channel_id=1, source_target_pairs={{0,0},{1,1},{2,2},{3,3},{4,4},{5,5},{6,6},{7,7},{8,64},{9,65},{10,... | collective-permute-start | bytes 786440 | tf_op jit(solution)/shard_map/ppermute | solution.py:41
  202.1 2.3 convolution_subtract_fusion.1
  204.5 4.5 %fusion.16 = bf16[128,1024]{0,1:T(8,128)(2,1)S(1)} fusion(bf16[2,1024,1024]{2,1,0:T(8,128)(2,1)} %all-gather.5.cloned.1.call-done, bf16[1024,128]{1,0:T(8,128)(2,1)} %copy-done.2, bf16[1024,2048]{1,0:T(8,128)(2,1)} %copy-done, bf16[2,1024,128]{2,1,0:T(8,128)(2,1)} %param.12), kind=kOutput, calls=%fused_computation.19 | convolution fusion | flops 537395200 | bytes 4980736 | tf_op jit(solution)/shard_map/dot_general | solution.py:10
  209.0 1.8 pad_maximum_fusion
  210.8 1.5 convolution_subtract_fusion
  212.3 33.1 %collective-permute-done.1 = bf16[1024,128]{1,0:T(8,128)(2,1)S(1)} collective-permute-done((bf16[1024,128]{1,0:T(8,128)(2,1)}, bf16[1024,128]{1,0:T(8,128)(2,1)S(1)}, u32[]{:S(2)}, u32[]{:S(2)}) %collective-permute-start.1) | collective-permute-done | bytes 262176 | tf_op jit(solution)/shard_map/ppermute | solution.py:42
  245.4 0.7 fusion.36
  246.2 4.4 %collective-permute-done = bf16[1024,128]{1,0:T(8,128)(2,1)} collective-permute-done((bf16[1024,128]{1,0:T(8,128)(2,1)S(1)}, bf16[1024,128]{1,0:T(8,128)(2,1)}, u32[]{:S(2)}, u32[]{:S(2)}) %collective-permute-start) | collective-permute-done | bytes 262176 | tf_op jit(solution)/shard_map/ppermute | solution.py:41
  250.6 2.5 fusion.15
  (16 shorter events, 2.2 us)
Async XLA Ops:
  7.2 65.7 %all-gather.5.cloned.1.call-start = ((), (), s32[]{:S(2)}) async-start(), calls=%async_computation.2 | async-start | bytes 4718592 | tf_op jit(solution)/shard_map/all_gather | solution.py:29
  7.9 152.5 %all-gather.3.cloned.1.call-start = ((), (), s32[]{:S(2)}) async-start(), calls=%async_computation.1 | async-start | bytes 6389760 | tf_op jit(solution)/shard_map/all_gather | solution.py:32
  75.2 127.0 %copy-start.2 = (bf16[1024,128]{1,0:T(8,128)(2,1)}, bf16[1024,128]{1,0:T(8,128)(2,1)S(1)}, u32[]{:S(2)}) copy-start(bf16[1024,128]{1,0:T(8,128)(2,1)S(1)} %fusion.17) | copy-start | bytes 786436
  178.7 2.1 copy-start
  192.8 52.7 %collective-permute-start.1 = (bf16[1024,128]{1,0:T(8,128)(2,1)}, bf16[1024,128]{1,0:T(8,128)(2,1)S(1)}, u32[]{:S(2)}, u32[]{:S(2)}) collective-permute-start(bf16[1024,128]{1,0:T(8,128)(2,1)} %dynamic-slice_bitcast_fusion), channel_id=1, source_target_pairs={{0,0},{1,1},{2,2},{3,3},{4,4},{5,5},{6,6},{7,7},{8,64},{9,65},{10,... | collective-permute-start | bytes 786440 | tf_op jit(solution)/shard_map/ppermute | solution.py:42
  198.2 52.3 %collective-permute-start = (bf16[1024,128]{1,0:T(8,128)(2,1)S(1)}, bf16[1024,128]{1,0:T(8,128)(2,1)}, u32[]{:S(2)}, u32[]{:S(2)}) collective-permute-start(bf16[1024,128]{1,0:T(8,128)(2,1)S(1)} %constant_dynamic-slice_fusion), channel_id=1, source_target_pairs={{0,0},{1,1},{2,2},{3,3},{4,4},{5,5},{6,6},{7,7},{8,64},{9,65},{10,... | collective-permute-start | bytes 786440 | tf_op jit(solution)/shard_map/ppermute | solution.py:41
  210.8 39.7 %copy-start.1 = (bf16[1024,2048]{1,0:T(8,128)(2,1)S(1)}, bf16[1024,2048]{1,0:T(8,128)(2,1)}, u32[]{:S(2)}) copy-start(bf16[1024,2048]{1,0:T(8,128)(2,1)} %copy-done) | copy-start | bytes 12582916
  210.8 39.7 %copy-start.3 = (bf16[1024,128]{1,0:T(8,128)(2,1)S(1)}, bf16[1024,128]{1,0:T(8,128)(2,1)}, u32[]{:S(2)}) copy-start(bf16[1024,128]{1,0:T(8,128)(2,1)} %param.10) | copy-start | bytes 786436
Sparse Core Ops, SparseCore 0:
  10.1 62.7 all-gather.4
  76.8 83.5 all-gather.2
where the time goes:
time: 261 us; the launch traced here: 260 us
  waiting for transfers between devices  168 us (64%)
  matrix products  29.4 us (11%)
  blocking collectives  18.1 us (7%)
  local copies, waits for them, and re-layouts  17.6 us (7%)
  between operations  14.1 us (5%)
  starting transfers between devices  8.8 us (3%)
  other arithmetic  3.86 us (1%)
    all_gather x1, waiting for transfers between devices, per_device(): panels = lax.all_gather(panels, ('y', 'core', 'vox'), axis=1, tiled=True)  85.2 us
    all_gather x1, waiting for transfers between devices, per_device(): whole = lax.all_gather(inverses, 'row', axis=1, tiled=True)  44.6 us
    ppermute x1, waiting for transfers between devices, per_device(): lax.ppermute(lax.dynamic_slice_in_dim(second_low, start, rest_cols, 1), a...  33.1 us
    dot_general x8, matrix products, contract(): lax.dot_general(left, right, (dims, ((), ())), preferred_element_type=jnp...  29.4 us
    all_to_all x1, blocking collectives, gather_small(): out = lax.all_to_all(jnp.tile(block, (size, 1)), axis, 0, 0, tiled=True)  18.1 us
    unnamed x9, local copies, waits for them, and re-layouts  8.24 us
    ppermute x1, starting transfers between devices, per_device(): lax.ppermute(lax.dynamic_slice_in_dim(second_low, start, rest_cols, 1), a...  5.48 us
  transfers between devices with their start and end apart: 4, of which 4 were waited for; matrix products, arithmetic and copies ran while one was open for 6% of the time, Pallas kernels for 0%

commit v1 on v0

--- a/solution.py
+++ b/solution.py
@@ -26,7 +26,24 @@
     width = panel_low.shape[1]
     rest_cols = gram_rest.shape[1]
     bf16 = jnp.bfloat16
-    whole = lax.all_gather(inverses, "row", axis=1, tiled=True)
+
+    def pair_target_for(panel, ax_name):
+        sides = lax.axis_size(ax_name)
+        crops = tuple(((s, (s + 1) % sides) for s in range(sides)))
+        lanes = tuple(((s, (s - 1) % sides) for s in range(sides)))
+        inter, formed = ([panel], [panel])
+        for _ in range(sides // 2):
+            met_up = lax.ppermute(inter[-1], ax_name, crops)
+            inter.append(met_up)
+        for _ in tuple(range((sides - 1) // 2)):
+            kept_arr = lax.ppermute(formed[-1], axis_name=ax_name, perm=lanes)
+            formed.append(kept_arr)
+        ready = jnp.concatenate([*inter[::-1], *formed[1:]], axis=1)
+        return jnp.roll(
+            ready, shift=(lax.axis_index(ax_name) - sides // 2) * panel.shape[1], axis=1
+        )
+
+    whole = pair_target_for(inverses, ax_name="row")
     top = gather_small(panel_top.T, "row", rows).transpose(1, 0, 2).reshape(width, -1)
     panels = jnp.stack([top, panel_low.T, panel_next.T])
     panels = lax.all_gather(panels, ("y", "core", "vox"), axis=1, tiled=True)

time: 261 us -> 210 us (0.80)
  waiting for transfers between devices: 168 us -> 95.4 us
  starting transfers between devices: 8.8 us -> 32.6 us
  matrix products: 29.4 us -> 25.2 us
  local copies, waits for them, and re-layouts: 17.6 us -> 20.9 us
    all_gather x1, waiting for transfers between devices: 85.2 us -> 19.8 us  [per_device(): panels = lax.all_gather(panels, ('y', 'core', 'vox'), axis=1, tiled=True)]
    all_gather x1 -> x0, waiting for transfers between devices: 44.6 us -> none  [per_device(): whole = lax.all_gather(inverses, 'row', axis=1, tiled=True)]
    ppermute x0 -> x7, waiting for transfers between devices: none -> 32.1 us  [the longest x4 32.1 us: pair_target_for(): met_up = lax.ppermute(inter[-1], ax_name, crops)]
    ppermute x0 -> x7, starting transfers between devices: none -> 23.7 us  [the longest x3 15.5 us: pair_target_for(): kept_arr = lax.ppermute(formed[-1], axis_name=ax_name, perm=lanes)]
    ppermute x1, waiting for transfers between devices: 33.1 us -> 38.6 us  [per_device(): lax.ppermute(lax.dynamic_slice_in_dim(second_low, start, rest_cols, 1), a...]
    dot_general x8, matrix products: 29.4 us -> 25.2 us  [contract(): lax.dot_general(left, right, (dims, ((), ())), preferred_element_type=jnp...]
    unnamed x9 -> x32, local copies, waits for them, and re-layouts: 8.24 us -> 12.1 us
  transfers between devices with their start and end apart: 4 -> 10, of which waited for: 4 -> 7; matrix products, arithmetic and copies ran while one was open for 6% -> 4% of each run, Pallas kernels for 0% -> 0%
where the time goes in v1:
time: 210 us
  waiting for transfers between devices  95.4 us (45%)
  starting transfers between devices  32.6 us (16%)
  matrix products  25.2 us (12%)
  local copies, waits for them, and re-layouts  20.9 us (10%)
  blocking collectives  18.1 us (9%)
  between operations  14.4 us (7%)
  other arithmetic  2.91 us (1%)
    ppermute x1, waiting for transfers between devices, per_device(): lax.ppermute(lax.dynamic_slice_in_dim(second_low, start, rest_cols, 1), a...  38.6 us
    ppermute x4, waiting for transfers between devices, pair_target_for(): met_up = lax.ppermute(inter[-1], ax_name, crops)  32.1 us
    dot_general x8, matrix products, contract(): lax.dot_general(left, right, (dims, ((), ())), preferred_element_type=jnp...  25.2 us
    all_gather x1, waiting for transfers between devices, per_device(): panels = lax.all_gather(panels, ('y', 'core', 'vox'), axis=1, tiled=True)  19.8 us
    all_to_all x1, blocking collectives, gather_small(): out = lax.all_to_all(jnp.tile(block, (size, 1)), axis, 0, 0, tiled=True)  18.1 us
    ppermute x3, starting transfers between devices, pair_target_for(): kept_arr = lax.ppermute(formed[-1], axis_name=ax_name, perm=lanes)  15.5 us
    unnamed x32, local copies, waits for them, and re-layouts  12.1 us
    ppermute x4, starting transfers between devices, pair_target_for(): met_up = lax.ppermute(inter[-1], ax_name, crops)  8.2 us
  transfers between devices with their start and end apart: 10, of which 7 were waited for; matrix products, arithmetic and copies ran while one was open for 4% of the time, Pallas kernels for 0%

profile of v1, /device:TPU:16, one launch (start us, length us, event | category | flops | bytes accessed | tf_op | source)
XLA Modules:
  0.0 209.5 jit_solution(17943260075409718263)
XLA Ops:
  7.9 18.1 %all_to_all.6 = bf16[8,16,128]{2,1,0:T(8,128)(2,1)S(1)} all-to-all(bf16[8,16,128]{2,1,0:T(8,128)(2,1)S(1)} %tile.2), channel_id=1, replica_groups=mesh['row'=8,'y'=8,'core'=2,'vox'=4] {'row'}, dimensions={0} | all-to-all | bytes 65536 | tf_op jit(solution)/shard_map/all_to_all | solution.py:14
  27.5 2.5 %collective-permute-start = (bf16[2,128,1024]{2,1,0:T(8,128)(2,1)}, bf16[2,128,1024]{2,1,0:T(8,128)(2,1)S(1)}, u32[]{:S(2)}, u32[]{:S(2)}) collective-permute-start(bf16[2,128,1024]{2,1,0:T(8,128)(2,1)} %param.11), channel_id=1, source_target_pairs={{0,64},{64,128},{128,192},{192,256},{256,320},{320,384},{384,448},... | collective-permute-start | bytes 1572872 | tf_op jit(solution)/shard_map/ppermute | solution.py:36
  30.0 13.1 %collective-permute-done = bf16[2,128,1024]{2,1,0:T(8,128)(2,1)S(1)} collective-permute-done((bf16[2,128,1024]{2,1,0:T(8,128)(2,1)}, bf16[2,128,1024]{2,1,0:T(8,128)(2,1)S(1)}, u32[]{:S(2)}, u32[]{:S(2)}) %collective-permute-start) | collective-permute-done | bytes 524320 | tf_op jit(solution)/shard_map/ppermute | solution.py:36
  43.1 1.9 collective-permute-start.1
  45.0 5.1 %collective-permute-start.4 = (bf16[2,128,1024]{2,1,0:T(8,128)(2,1)}, bf16[2,128,1024]{2,1,0:T(8,128)(2,1)S(1)}, u32[]{:S(2)}, u32[]{:S(2)}) collective-permute-start(bf16[2,128,1024]{2,1,0:T(8,128)(2,1)} %param.11), channel_id=1, source_target_pairs={{0,448},{64,0},{128,64},{192,128},{256,192},{320,256},{384,320},{4... | collective-permute-start | bytes 1572872 | tf_op jit(solution)/shard_map/ppermute | solution.py:39
  50.1 7.3 %collective-permute-done.1 = bf16[2,128,1024]{2,1,0:T(8,128)(2,1)S(1)} collective-permute-done((bf16[2,128,1024]{2,1,0:T(8,128)(2,1)S(1)}, bf16[2,128,1024]{2,1,0:T(8,128)(2,1)S(1)}, u32[]{:S(2)}, u32[]{:S(2)}) %collective-permute-start.1) | collective-permute-done | bytes 524320 | tf_op jit(solution)/shard_map/ppermute | solution.py:36
  57.5 1.9 collective-permute-start.2
  59.4 5.1 %collective-permute-start.5 = (bf16[2,128,1024]{2,1,0:T(8,128)(2,1)S(1)}, bf16[2,128,1024]{2,1,0:T(8,128)(2,1)S(1)}, u32[]{:S(2)}, u32[]{:S(2)}) collective-permute-start(bf16[2,128,1024]{2,1,0:T(8,128)(2,1)S(1)} %collective-permute-done.4), channel_id=1, source_target_pairs={{0,448},{64,0},{128,64},{192,128},{256,192},{320,256},{384,320},{4... | collective-permute-start | bytes 1572872 | tf_op jit(solution)/shard_map/ppermute | solution.py:39
  64.5 6.4 %collective-permute-done.2 = bf16[2,128,1024]{2,1,0:T(8,128)(2,1)S(1)} collective-permute-done((bf16[2,128,1024]{2,1,0:T(8,128)(2,1)S(1)}, bf16[2,128,1024]{2,1,0:T(8,128)(2,1)S(1)}, u32[]{:S(2)}, u32[]{:S(2)}) %collective-permute-start.2) | collective-permute-done | bytes 524320 | tf_op jit(solution)/shard_map/ppermute | solution.py:36
  71.0 1.9 collective-permute-start.3
  72.9 5.3 %collective-permute-start.6 = (bf16[2,128,1024]{2,1,0:T(8,128)(2,1)S(1)}, bf16[2,128,1024]{2,1,0:T(8,128)(2,1)S(1)}, u32[]{:S(2)}, u32[]{:S(2)}) collective-permute-start(bf16[2,128,1024]{2,1,0:T(8,128)(2,1)S(1)} %collective-permute-done.5), channel_id=1, source_target_pairs={{0,448},{64,0},{128,64},{192,128},{256,192},{320,256},{384,320},{4... | collective-permute-start | bytes 1572872 | tf_op jit(solution)/shard_map/ppermute | solution.py:39
  78.2 5.3 %collective-permute-done.3 = bf16[2,128,1024]{2,1,0:T(8,128)(2,1)S(1)} collective-permute-done((bf16[2,128,1024]{2,1,0:T(8,128)(2,1)S(1)}, bf16[2,128,1024]{2,1,0:T(8,128)(2,1)S(1)}, u32[]{:S(2)}, u32[]{:S(2)}) %collective-permute-start.3) | collective-permute-done | bytes 524320 | tf_op jit(solution)/shard_map/ppermute | solution.py:36
  85.4 3.2 %copy-done.3 = bf16[2,2048,1024]{2,1,0:T(8,128)(2,1)} copy-done((bf16[2,2048,1024]{2,1,0:T(8,128)(2,1)}, bf16[2,2048,1024]{2,1,0:T(8,128)(2,1)S(1)}, u32[]{:S(2)}) %copy-start.3) | copy-done | bytes 8388632
  89.3 19.8 %all-gather.2.cloned.1.call-done = bf16[3,1024,1024]{2,1,0:T(8,128)(2,1)} async-done(((bf16[3,16,1024]{2,1,0:T(8,128)(2,1)}), bf16[3,1024,1024]{2,1,0:T(8,128)(2,1)}) %all-gather.2.cloned.1.call-update) | async-done | bytes 6291472 | tf_op jit(solution)/shard_map/all_gather | solution.py:49
  109.1 4.6 %slice.34 = bf16[2,1024,1024]{2,1,0:T(8,128)(2,1)} slice(bf16[3,1024,1024]{2,1,0:T(8,128)(2,1)} %all-gather.2.cloned.1.call-done), slice={[0:2], [0:1024], [0:1024]} | slice | bytes 8388608 | tf_op jit(solution)/shard_map/slice | solution.py:50
  113.7 6.2 %copy.17 = bf16[2,1024,1024]{1,2,0:T(8,128)(2,1)} copy(bf16[2,1024,1024]{2,1,0:T(8,128)(2,1)} %slice.34) | data formatting | bytes 8388608
  120.0 7.4 %convolution_convert_fusion = bf16[1024,2048]{1,0:T(8,128)(2,1)S(1)} fusion(bf16[1024,2048]{0,1:T(8,128)(2,1)} %bitcast.58, bf16[2,2048,1024]{2,1,0:T(8,128)(2,1)} %copy-done.3, s32[]{:T(128)S(6)} %select_n.22), kind=kOutput, calls=%fused_computation.2 | convolution fusion | flops 4297064448 | bytes 10485764 | tf_op jit(solution)/shard_map/dot_general | solution.py:10
  127.4 1.6 slice.35
  130.7 4.5 %fusion.16 = bf16[1024,128]{1,0:T(8,128)(2,1)S(1)} fusion(bf16[2,2048,1024]{2,1,0:T(8,128)(2,1)} %copy-done.3, s32[]{:T(128)S(6)} %add.35, s32[]{:T(128)S(6)} %select_n.22, bf16[1024,128]{1,0:T(8,128)(2,1)S(1)} %fusion.17, bf16[1024,2048]{1,0:T(8,128)(2,1)} %copy-done.1, bf16[2,1024,128]{2,1,0:T(8,128)(2,1)S(1)} %copy-done.5), kind=kOutput, calls=%fused_computation.19 | convolution fusion | flops 537395200 | bytes 4980744 | tf_op jit(solution)/shard_map/dot_general | solution.py:10
  135.2 8.0 %fusion.3 = bf16[1024,1024]{1,0:T(8,128)(2,1)S(1)} fusion(bf16[3,1024,1024]{2,1,0:T(8,128)(2,1)} %all-gather.2.cloned.1.call-done, bf16[2,2048,1024]{2,1,0:T(8,128)(2,1)} %copy-done.3, s32[]{:T(128)S(6)} %add.35, s32[]{:T(128)S(6)} %select_n.22, bf16[1024,2048]{1,0:T(8,128)(2,1)} %copy-done.1), kind=kOutput, calls=%fused_computation.7 | convolution fusion | flops 4299161600 | bytes 10485768 | tf_op jit(solution)/shard_map/dot_general | solution.py:10
  143.4 5.7 %collective-permute-start.8 = (bf16[1024,128]{1,0:T(8,128)(2,1)S(1)}, bf16[1024,128]{1,0:T(8,128)(2,1)S(1)}, u32[]{:S(2)}, u32[]{:S(2)}) collective-permute-start(bf16[1024,128]{1,0:T(8,128)(2,1)S(1)} %constant_dynamic-slice_fusion), channel_id=1, source_target_pairs={{0,0},{1,1},{2,2},{3,3},{4,4},{5,5},{6,6},{7,7},{8,64},{9,65},{10,... | collective-permute-start | bytes 786440 | tf_op jit(solution)/shard_map/ppermute | solution.py:59
  150.1 3.1 %collective-permute-start.7 = (bf16[1024,128]{1,0:T(8,128)(2,1)S(1)}, bf16[1024,128]{1,0:T(8,128)(2,1)S(1)}, u32[]{:S(2)}, u32[]{:S(2)}) collective-permute-start(bf16[1024,128]{1,0:T(8,128)(2,1)S(1)} %constant_dynamic-slice_fusion.1), channel_id=1, source_target_pairs={{0,0},{1,1},{2,2},{3,3},{4,4},{5,5},{6,6},{7,7},{8,64},{9,65},{10,... | collective-permute-start | bytes 786440 | tf_op jit(solution)/shard_map/ppermute | solution.py:58
  156.9 38.6 %collective-permute-done.8 = bf16[1024,128]{1,0:T(8,128)(2,1)S(1)} collective-permute-done((bf16[1024,128]{1,0:T(8,128)(2,1)S(1)}, bf16[1024,128]{1,0:T(8,128)(2,1)S(1)}, u32[]{:S(2)}, u32[]{:S(2)}) %collective-permute-start.8) | collective-permute-done | bytes 262176 | tf_op jit(solution)/shard_map/ppermute | solution.py:59
  196.3 4.9 %collective-permute-done.7 = bf16[1024,128]{1,0:T(8,128)(2,1)S(1)} collective-permute-done((bf16[1024,128]{1,0:T(8,128)(2,1)S(1)}, bf16[1024,128]{1,0:T(8,128)(2,1)S(1)}, u32[]{:S(2)}, u32[]{:S(2)}) %collective-permute-start.7) | collective-permute-done | bytes 262176 | tf_op jit(solution)/shard_map/ppermute | solution.py:58
  (50 shorter events, 13.5 us)
Async XLA Ops:
  7.2 102.0 %all-gather.2.cloned.1.call-start = ((), (), s32[]{:S(2)}) async-start(), calls=%async_computation.1 | async-start | bytes 6389760 | tf_op jit(solution)/shard_map/all_gather | solution.py:49
  27.5 15.6 %collective-permute-start = (bf16[2,128,1024]{2,1,0:T(8,128)(2,1)}, bf16[2,128,1024]{2,1,0:T(8,128)(2,1)S(1)}, u32[]{:S(2)}, u32[]{:S(2)}) collective-permute-start(bf16[2,128,1024]{2,1,0:T(8,128)(2,1)} %param.11), channel_id=1, source_target_pairs={{0,64},{64,128},{128,192},{192,256},{256,320},{320,384},{384,448},... | collective-permute-start | bytes 1572872 | tf_op jit(solution)/shard_map/ppermute | solution.py:36
  43.1 14.4 %collective-permute-start.1 = (bf16[2,128,1024]{2,1,0:T(8,128)(2,1)S(1)}, bf16[2,128,1024]{2,1,0:T(8,128)(2,1)S(1)}, u32[]{:S(2)}, u32[]{:S(2)}) collective-permute-start(bf16[2,128,1024]{2,1,0:T(8,128)(2,1)S(1)} %collective-permute-done), channel_id=1, source_target_pairs={{0,64},{64,128},{128,192},{192,256},{256,320},{320,384},{384,448},... | collective-permute-start | bytes 1572872 | tf_op jit(solution)/shard_map/ppermute | solution.py:36
  45.0 14.4 %collective-permute-start.4 = (bf16[2,128,1024]{2,1,0:T(8,128)(2,1)}, bf16[2,128,1024]{2,1,0:T(8,128)(2,1)S(1)}, u32[]{:S(2)}, u32[]{:S(2)}) collective-permute-start(bf16[2,128,1024]{2,1,0:T(8,128)(2,1)} %param.11), channel_id=1, source_target_pairs={{0,448},{64,0},{128,64},{192,128},{256,192},{320,256},{384,320},{4... | collective-permute-start | bytes 1572872 | tf_op jit(solution)/shard_map/ppermute | solution.py:39
  57.5 13.5 %collective-permute-start.2 = (bf16[2,128,1024]{2,1,0:T(8,128)(2,1)S(1)}, bf16[2,128,1024]{2,1,0:T(8,128)(2,1)S(1)}, u32[]{:S(2)}, u32[]{:S(2)}) collective-permute-start(bf16[2,128,1024]{2,1,0:T(8,128)(2,1)S(1)} %collective-permute-done.1), channel_id=1, source_target_pairs={{0,64},{64,128},{128,192},{192,256},{256,320},{320,384},{384,448},... | collective-permute-start | bytes 1572872 | tf_op jit(solution)/shard_map/ppermute | solution.py:36
  59.4 13.5 %collective-permute-start.5 = (bf16[2,128,1024]{2,1,0:T(8,128)(2,1)S(1)}, bf16[2,128,1024]{2,1,0:T(8,128)(2,1)S(1)}, u32[]{:S(2)}, u32[]{:S(2)}) collective-permute-start(bf16[2,128,1024]{2,1,0:T(8,128)(2,1)S(1)} %collective-permute-done.4), channel_id=1, source_target_pairs={{0,448},{64,0},{128,64},{192,128},{256,192},{320,256},{384,320},{4... | collective-permute-start | bytes 1572872 | tf_op jit(solution)/shard_map/ppermute | solution.py:39
  71.0 12.6 %collective-permute-start.3 = (bf16[2,128,1024]{2,1,0:T(8,128)(2,1)S(1)}, bf16[2,128,1024]{2,1,0:T(8,128)(2,1)S(1)}, u32[]{:S(2)}, u32[]{:S(2)}) collective-permute-start(bf16[2,128,1024]{2,1,0:T(8,128)(2,1)S(1)} %collective-permute-done.2), channel_id=1, source_target_pairs={{0,64},{64,128},{128,192},{192,256},{256,320},{320,384},{384,448},... | collective-permute-start | bytes 1572872 | tf_op jit(solution)/shard_map/ppermute | solution.py:36
  72.9 12.3 %copy-start = (bf16[2,128,1024]{2,1,0:T(8,128)(2,1)S(1)}, bf16[2,128,1024]{2,1,0:T(8,128)(2,1)}, u32[]{:S(2)}) copy-start(bf16[2,128,1024]{2,1,0:T(8,128)(2,1)} %param.11) | copy-start | bytes 1572868
  72.9 12.0 %collective-permute-start.6 = (bf16[2,128,1024]{2,1,0:T(8,128)(2,1)S(1)}, bf16[2,128,1024]{2,1,0:T(8,128)(2,1)S(1)}, u32[]{:S(2)}, u32[]{:S(2)}) collective-permute-start(bf16[2,128,1024]{2,1,0:T(8,128)(2,1)S(1)} %collective-permute-done.5), channel_id=1, source_target_pairs={{0,448},{64,0},{128,64},{192,128},{256,192},{320,256},{384,320},{4... | collective-permute-start | bytes 1572872 | tf_op jit(solution)/shard_map/ppermute | solution.py:39
  83.7 4.9 %copy-start.4 = (bf16[2,1024,128]{2,1,0:T(8,128)(2,1)S(1)}, bf16[2,1024,128]{2,1,0:T(8,128)(2,1)}, u32[]{:S(2)}) copy-start(bf16[2,1024,128]{2,1,0:T(8,128)(2,1)} %param.12) | copy-start | bytes 1572868
  85.4 3.2 %copy-start.3 = (bf16[2,2048,1024]{2,1,0:T(8,128)(2,1)}, bf16[2,2048,1024]{2,1,0:T(8,128)(2,1)S(1)}, u32[]{:S(2)}) copy-start(bf16[2,2048,1024]{2,1,0:T(8,128)(2,1)S(1)} %constant_dynamic-update-slice_fusion) | copy-start | bytes 25165828
  120.0 10.0 %copy-start.6 = (bf16[1024,128]{1,0:T(8,128)(2,1)S(1)}, bf16[1024,128]{1,0:T(8,128)(2,1)}, u32[]{:S(2)}) copy-start(bf16[1024,128]{1,0:T(8,128)(2,1)} %param.13) | copy-start | bytes 786436
  127.4 2.6 %copy-start.1 = (bf16[1024,2048]{1,0:T(8,128)(2,1)}, bf16[1024,2048]{1,0:T(8,128)(2,1)S(1)}, u32[]{:S(2)}) copy-start(bf16[1024,2048]{1,0:T(8,128)(2,1)S(1)} %convolution_convert_fusion) | copy-start | bytes 12582916
  127.4 3.3 %copy-start.5 = (bf16[2,1024,128]{2,1,0:T(8,128)(2,1)S(1)}, bf16[2,1024,128]{2,1,0:T(8,128)(2,1)}, u32[]{:S(2)}) copy-start(bf16[2,1024,128]{2,1,0:T(8,128)(2,1)} %param.12) | copy-start | bytes 1572868
  143.3 57.8 %copy-start.2 = (bf16[1024,2048]{1,0:T(8,128)(2,1)S(1)}, bf16[1024,2048]{1,0:T(8,128)(2,1)}, u32[]{:S(2)}) copy-start(bf16[1024,2048]{1,0:T(8,128)(2,1)} %copy-done.1) | copy-start | bytes 12582916
  143.4 57.8 %copy-start.7 = (bf16[1024,128]{1,0:T(8,128)(2,1)S(1)}, bf16[1024,128]{1,0:T(8,128)(2,1)}, u32[]{:S(2)}) copy-start(bf16[1024,128]{1,0:T(8,128)(2,1)} %param.10) | copy-start | bytes 786436
  143.4 52.2 %collective-permute-start.8 = (bf16[1024,128]{1,0:T(8,128)(2,1)S(1)}, bf16[1024,128]{1,0:T(8,128)(2,1)S(1)}, u32[]{:S(2)}, u32[]{:S(2)}) collective-permute-start(bf16[1024,128]{1,0:T(8,128)(2,1)S(1)} %constant_dynamic-slice_fusion), channel_id=1, source_target_pairs={{0,0},{1,1},{2,2},{3,3},{4,4},{5,5},{6,6},{7,7},{8,64},{9,65},{10,... | collective-permute-start | bytes 786440 | tf_op jit(solution)/shard_map/ppermute | solution.py:59
  150.1 51.0 %collective-permute-start.7 = (bf16[1024,128]{1,0:T(8,128)(2,1)S(1)}, bf16[1024,128]{1,0:T(8,128)(2,1)S(1)}, u32[]{:S(2)}, u32[]{:S(2)}) collective-permute-start(bf16[1024,128]{1,0:T(8,128)(2,1)S(1)} %constant_dynamic-slice_fusion.1), channel_id=1, source_target_pairs={{0,0},{1,1},{2,2},{3,3},{4,4},{5,5},{6,6},{7,7},{8,64},{9,65},{10,... | collective-permute-start | bytes 786440 | tf_op jit(solution)/shard_map/ppermute | solution.py:58
Sparse Core Ops, SparseCore 0:
  27.6 81.4 all-gather.1
